TPU v7x, 512 devices: a whole 4x8x8 slice. The times are simulated.
512 devices in a mesh: gx: 32 (over z, x), gy: 16 (over y, core).
Axes of the slice: x: 4, y: 8, z: 8, core: 2. Of those that a mesh axis runs over, the one named last changes fastest.
Arguments:
- eigen: float32 [256, 256, 256], P('gx', 'gy'), may hold values from -6 to 6
- seg_vec: float32 [6, 32, 16, 2048], P(None, 'gx', 'gy'), may hold values from -5 to 5
- seg_off: float32 [3, 32, 16, 2048], P(None, 'gx', 'gy'), may hold values from 0 to 1
- seg_cell: int32 [32, 16, 2048], P('gx', 'gy'), may hold values from 0 to 32767
- blk_count: int32 [32, 16, 16], P('gx', 'gy'), may hold values from 0 to 128, as said below
- pair_list: int32 [32, 16, 16, 8], P('gx', 'gy'), may hold values from 0 to 143, as said below
Outputs:
- stress_field: float32 [256, 256, 256], P('gx', 'gy')
- seg_force: float32 [3, 32, 16, 2048], P(None, 'gx', 'gy')
Inputs may be any that keep to these rules, and one draw needn't show every extreme that they name: `blk_count`: A block's live segments fill its first slots; at least one device holds 16 full blocks of 128; every device holds a block with segments. `pair_list`: the 8 entries of one block are distinct.
All inputs are finite; a program needn't handle non-finite values.
Results may differ from a plain program's by a relative error of at most 0.0003.
Values sent between devices are 32-bit elements; how exact they have to be, the bound alone decides.
A program may use at most 64 MiB of HBM per device.

v0:
```python
import functools
import math

import jax
import jax.numpy as jnp
import ml_dtypes
import numpy as np
from jax import lax
from jax.experimental import pallas as pl
from jax.experimental.pallas import tpu as pltpu
from jax.sharding import PartitionSpec as P

nu_copper = 0.34
core_sq = 4.0
pair_scale = 4.0

MESH = pl.DeviceIdType.MESH
ROWS = 9
LANES = 128


def cas_table(length):
    steps = np.arange(length)
    angle = (steps[:, None] * steps[None, :] % length) * (2.0 * math.pi / length)
    table = np.cos(angle) + np.sin(angle)
    high = table.astype(ml_dtypes.bfloat16)
    low = (table - high.astype(np.float64)).astype(ml_dtypes.bfloat16)
    return np.stack([high, low])


def parts(x):
    high = x.astype(jnp.bfloat16)
    return high, (x - high.astype(jnp.float32)).astype(jnp.bfloat16)


def mm(a, b):
    return jnp.dot(a, b, preferred_element_type=jnp.float32)


def times_table(x, tab):
    high, low = parts(x)
    return mm(high, tab[0]) + (mm(low, tab[0]) + mm(high, tab[1]))


def table_times(tab, x):
    high, low = parts(x)
    return mm(tab[0], high) + (mm(tab[0], low) + mm(tab[1], high))


def swap_blocks(tiles, width):
    count = len(tiles)
    lane = lax.broadcasted_iota(jnp.int32, (8, LANES), 1) // width
    tiles = list(tiles)
    bit = 1
    while bit < count:
        keep = (lane & bit) == 0
        shift = bit * width
        for i in range(count):
            if i & bit:
                continue
            a, c = tiles[i], tiles[i | bit]
            tiles[i] = jnp.where(keep, a, pltpu.roll(c, shift, 1))
            tiles[i | bit] = jnp.where(keep, pltpu.roll(a, LANES - shift, 1), c)
        bit *= 2
    return tiles


def kernel(
    nx, ny, eigen_hbm, vec_hbm, off_hbm, cell_hbm, count_ref, pair_ref, tab_hbm,
    stress_hbm, force_hbm,
    eigen, vec, off, cell, tab, send1, recv1, send2, recv2, send3, recv3, send4, recv4,
    mid_a, mid_b, gain, source, pool, by_block, own_wide, far_wide, pull, hot, stress, force,
    load_sem, send_sem, recv_sem, store_sem,
):
    me_x = lax.axis_index("gx")
    me_y = lax.axis_index("gy")

    barrier = pltpu.get_barrier_semaphore()

    def greet_x(i, _):
        pl.semaphore_signal(barrier, inc=1, device_id={"gx": lax.rem(me_x + i, nx)}, device_id_type=MESH)
        return 0

    def greet_y(i, _):
        pl.semaphore_signal(barrier, inc=1, device_id={"gy": lax.rem(me_y + i, ny)}, device_id_type=MESH)
        return 0

    lax.fori_loop(1, nx, greet_x, 0)
    lax.fori_loop(1, ny, greet_y, 0)
    for dx in (-1, 1):
        for dy in (-1, 1):
            peer = {"gx": lax.rem(me_x + dx + nx, nx), "gy": lax.rem(me_y + dy + ny, ny)}
            pl.semaphore_signal(barrier, inc=1, device_id=peer, device_id_type=MESH)

    loads = [
        pltpu.make_async_copy(src, dst, load_sem.at[n])
        for n, (src, dst) in enumerate(
            (
                (eigen_hbm.at[:, pl.ds(0, LANES)], eigen.at[0]),
                (eigen_hbm.at[:, pl.ds(LANES, LANES)], eigen.at[1]),
                (tab_hbm, tab),
                (vec_hbm, vec),
                (off_hbm, off),
                (cell_hbm, cell),
            )
        )
    ]
    for load in loads:
        load.start()
    for load in loads[:3]:
        load.wait()

    lines = jnp.concatenate(
        [
            jnp.concatenate([eigen[h, pl.ds(y, 8, stride=16), :] for h in range(2)], axis=1)
            for y in range(16)
        ],
        axis=0,
    )
    zeta = times_table(lines, tab)
    for h in range(2):
        tiles = [zeta[y * 8 : y * 8 + 8, h * LANES : (h + 1) * LANES] for y in range(16)]
        for j, tile in enumerate(swap_blocks(tiles, 8)):
            send1[h * 16 + j] = tile

    pl.semaphore_wait(barrier, nx - 1 + ny - 1 + 4)

    def exchange(axis, me, count, send, recv, stage):
        def push(i, _):
            peer = lax.rem(me + i, count)
            pltpu.make_async_remote_copy(
                src_ref=send.at[peer], dst_ref=recv.at[me], send_sem=send_sem.at[stage],
                recv_sem=recv_sem.at[stage], device_id={axis: peer}, device_id_type=MESH,
            ).start()
            return 0

        lax.fori_loop(1, count, push, 0)
        recv[me] = send[me]

    def arrived(buffer, count, stage):
        whole = buffer.at[pl.ds(0, count)]
        pltpu.make_async_copy(whole, whole, recv_sem.at[stage]).wait()

    def left(buffer, count, stage):
        whole = buffer.at[pl.ds(0, count)]
        pltpu.make_async_copy(whole, whole, send_sem.at[stage]).wait()

    exchange("gx", me_x, nx, send1, recv1, 0)

    for load in loads[3:]:
        load.wait()
    row_id = lax.broadcasted_iota(jnp.int32, (16, LANES), 0)
    lane_id = lax.broadcasted_iota(jnp.int32, (16, LANES), 1)
    counts = jnp.zeros((16, LANES), jnp.int32)
    for b in range(16):
        counts = jnp.where(row_id == b, count_ref[b], counts)
    live = jnp.where(lane_id < counts, 1.0, 0.0)
    place = cell[...]
    spots = (place >> 12, (place >> 8) & 15, place & 255)
    for k in range(3):
        source[k] = spots[k].astype(jnp.float32) + off[k]
        source[3 + k] = vec[k] * live
        source[6 + k] = vec[3 + k]
    for dx in (-1, 0, 1):
        for dy in (-1, 0, 1):
            if dx == 0 and dy == 0:
                continue
            peer = {"gx": lax.rem(me_x + dx + nx, nx), "gy": lax.rem(me_y + dy + ny, ny)}
            pltpu.make_async_remote_copy(
                src_ref=source, dst_ref=pool.at[(1 - dx) * 3 + (1 - dy)], send_sem=send_sem.at[4],
                recv_sem=recv_sem.at[4], device_id=peer, device_id_type=MESH,
            ).start()
    for r in range(ROWS):
        pool[4, r] = source[r]

    for r in range(ROWS):
        rows = source[r]
        for b in range(16):
            by_block[b, pl.ds(r, 1), :] = rows[b : b + 1]

    def wave(index):
        sine = 2.0 * jnp.sin(index.astype(jnp.float32) * (math.pi / 256.0))
        return sine * sine

    lane_row = lax.broadcasted_iota(jnp.int32, (8, LANES), 1)
    freq_z = me_x * 8 + (lane_row >> 4)
    freq_x = me_y * 16 + (lane_row & 15)
    wave_x, wave_z = wave(freq_x), wave(freq_z)
    both = wave_x + wave_z
    product = 2.0 / (1.0 - nu_copper) * wave_x * wave_z
    corner = (freq_x == 0) & (freq_z == 0)

    def fill_gain(i, _):
        freq_y = i * 8 + lax.broadcasted_iota(jnp.int32, (8, LANES), 0)
        total = both + wave(freq_y)
        safe = jnp.where(corner & (freq_y == 0), 1.0, total)
        inverse = 1.0 / safe
        gain[pl.ds(pl.multiple_of(i * 8, 8), 8), :] = (-2.0 / 256.0**3) * (
            1.0 - both * inverse + product * inverse * inverse
        )
        return 0

    lax.fori_loop(0, 32, fill_gain, 0)

    spot = ((place >> 7) & 1) * 128 + ((place >> 8) & 15) * 8 + (place >> 12)
    for b in range(16):
        want = jnp.broadcast_to(spot[b : b + 1], (256, LANES))
        at = lax.broadcasted_iota(jnp.int32, (256, LANES), 0)
        hot[:, b * LANES : (b + 1) * LANES] = jnp.where(want == at, 1.0, 0.0).astype(jnp.bfloat16)

    arrived(recv1, nx - 1, 0)
    held = recv1[...].reshape(256, LANES)
    along_x = times_table(held.T, tab)
    for h in range(2):
        mid_a[h] = along_x[:, h * LANES : (h + 1) * LANES]
    for h in range(2):
        for s in range(2):
            tiles = [mid_a[h, pl.ds(s * 64 + c, 8, stride=8), :] for c in range(8)]
            for j, tile in enumerate(swap_blocks(tiles, 16)):
                send2[h * 8 + j, s * 8 : s * 8 + 8, :] = tile
    exchange("gy", me_y, ny, send2, recv2, 1)

    arrived(pool, 8, 4)
    for p in range(3):
        for q in range(3):
            if p != 1:
                pool[p * 3 + q, 0] += (p - 1) * 8.0
            if q != 1:
                pool[p * 3 + q, 1] += (q - 1) * 16.0

    def pair_block(b, _):
        for n in range(8):
            partner = pair_ref[n, b]
            device = partner >> 4
            slot = partner & 15
            for r in range(ROWS):
                far_wide[n, r] = jnp.broadcast_to(pool[device, r, pl.ds(slot, 1), :], (8, LANES))
        columns = by_block[b].T
        for r in range(ROWS):
            own_wide[r] = jnp.broadcast_to(columns[:, r : r + 1], (LANES, LANES))

        def tile(i, _):
            rows = pl.ds(pl.multiple_of(i * 8, 8), 8)
            own = [own_wide[r, rows, :] for r in range(ROWS)]
            triple = [3.0 * own[3 + k] for k in range(3)]
            total = [jnp.zeros((8, LANES), jnp.float32) for _ in range(3)]
            for n in range(8):
                far = [far_wide[n, r] for r in range(ROWS)]
                delta = [own[k] - far[k] for k in range(3)]
                square = (delta[0] * delta[0] + core_sq) + (delta[1] * delta[1] + delta[2] * delta[2])
                inverse = lax.rsqrt(square)
                inv_two = inverse * inverse
                inv_three = inv_two * inverse
                burg_dot = own[3] * far[3] + own[4] * far[4] + own[5] * far[5]
                line_dot = own[6] * far[6] + own[7] * far[7] + own[8] * far[8]
                burg_own = triple[0] * delta[0] + triple[1] * delta[1] + triple[2] * delta[2]
                burg_far = far[3] * delta[0] + far[4] * delta[1] + far[5] * delta[2]
                weight = (line_dot * inv_three) * (burg_dot - (burg_own * burg_far) * inv_two)
                total = [total[k] + weight * delta[k] for k in range(3)]
            lane = lax.broadcasted_iota(jnp.int32, (8, LANES), 1)
            have = pull[rows, :]
            for k in range(3):
                have = jnp.where(lane == k * 16 + b, jnp.sum(total[k], axis=1, keepdims=True), have)
            pull[rows, :] = have
            return 0

        lax.fori_loop(0, 16, tile, 0)
        return 0

    pull[...] = jnp.zeros_like(pull)
    lax.fori_loop(0, 5, pair_block, 0)

    arrived(recv2, ny - 1, 1)
    spectrum = table_times(tab, recv2[...].reshape(256, LANES)) * gain[...]
    send3[...] = table_times(tab, spectrum).reshape(16, 16, LANES)
    exchange("gy", me_y, ny, send3, recv3, 2)
    lax.fori_loop(5, 10, pair_block, 0)

    arrived(recv3, ny - 1, 2)
    for h in range(2):
        for s in range(2):
            tiles = [recv3[h * 8 + j, s * 8 : s * 8 + 8, :] for j in range(8)]
            for c, tile in enumerate(swap_blocks(tiles, 16)):
                mid_b[h, pl.ds(s * 64 + c, 8, stride=8), :] = tile
    back_x = jnp.concatenate([mid_b[0], mid_b[1]], axis=1).T
    send4[...] = table_times(tab, back_x).reshape(32, 8, LANES)
    exchange("gx", me_x, nx, send4, recv4, 3)
    lax.fori_loop(10, 16, pair_block, 0)

    arrived(recv4, nx - 1, 3)
    halves = []
    for h in range(2):
        tiles = [recv4[h * 16 + j] for j in range(16)]
        halves.append(jnp.concatenate(swap_blocks(tiles, 8), axis=0))
    final = times_table(jnp.concatenate(halves, axis=1), tab)
    for h in range(2):
        for y in range(16):
            stress[h, pl.ds(y, 8, stride=16), :] = final[y * 8 : y * 8 + 8, h * LANES : (h + 1) * LANES]
    stores = [
        pltpu.make_async_copy(
            stress.at[h], stress_hbm.at[:, pl.ds(h * LANES, LANES)], store_sem.at[h]
        )
        for h in range(2)
    ]
    for store in stores:
        store.start()

    tall = jnp.concatenate([final[:, :LANES], final[:, LANES:]], axis=0).T
    high, low = parts(tall)
    depth = place & 127
    tau_rows = []
    for b in range(16):
        picked = hot[:, b * LANES : (b + 1) * LANES]
        lines_b = mm(high, picked) + mm(low, picked)
        at = lax.broadcasted_iota(jnp.int32, (LANES, LANES), 0)
        chosen = jnp.where(at == jnp.broadcast_to(depth[b : b + 1], (LANES, LANES)), lines_b, 0.0)
        tau_rows.append(jnp.sum(chosen, axis=0, keepdims=True))
    tau = jnp.concatenate(tau_rows, axis=0)
    pulled = pull[...].T
    burgers = [source[3 + k] for k in range(3)]
    tangent = [source[6 + k] for k in range(3)]
    for k in range(3):
        k1, k2 = (k + 1) % 3, (k + 2) % 3
        glide = burgers[k1] * tangent[k2] - burgers[k2] * tangent[k1]
        force[k] = pair_scale * pulled[k * 16 : k * 16 + 16] + tau * glide
    last = pltpu.make_async_copy(force, force_hbm, store_sem.at[2])
    last.start()
    left(send1, nx - 1, 0)
    left(send2, ny - 1, 1)
    left(send3, ny - 1, 2)
    left(send4, nx - 1, 3)
    left(pool, 8, 4)
    for store in stores:
        store.wait()
    last.wait()


def per_device(nx, ny, eigen, seg_vec, seg_off, seg_cell, blk_count, pair_list):
    f32, bf16 = jnp.float32, jnp.bfloat16
    tab = jnp.asarray(cas_table(256))
    hbm = pl.BlockSpec(memory_space=pl.ANY)
    smem = pl.BlockSpec(memory_space=pltpu.SMEM)
    vmem = pltpu.VMEM
    stress, force = pl.pallas_call(
        functools.partial(kernel, nx, ny),
        out_shape=(
            jax.ShapeDtypeStruct((128, 256), f32),
            jax.ShapeDtypeStruct((3, 16, LANES), f32),
        ),
        in_specs=[hbm, hbm, hbm, hbm, smem, smem, hbm],
        out_specs=(hbm, hbm),
        scratch_shapes=[
            vmem((2, 128, LANES), f32),
            vmem((6, 16, LANES), f32),
            vmem((3, 16, LANES), f32),
            vmem((16, LANES), jnp.int32),
            vmem((2, 256, 256), bf16),
            vmem((32, 8, LANES), f32),
            vmem((32, 8, LANES), f32),
            vmem((16, 16, LANES), f32),
            vmem((16, 16, LANES), f32),
            vmem((16, 16, LANES), f32),
            vmem((16, 16, LANES), f32),
            vmem((32, 8, LANES), f32),
            vmem((32, 8, LANES), f32),
            vmem((2, 128, LANES), f32),
            vmem((2, 128, LANES), f32),
            vmem((256, LANES), f32),
            vmem((ROWS, 16, LANES), f32),
            vmem((9, ROWS, 16, LANES), f32),
            vmem((16, 16, LANES), f32),
            vmem((ROWS, LANES, LANES), f32),
            vmem((8, ROWS, 8, LANES), f32),
            vmem((LANES, LANES), f32),
            vmem((256, 2048), bf16),
            vmem((2, 128, LANES), f32),
            vmem((3, 16, LANES), f32),
            pltpu.SemaphoreType.DMA((6,)),
            pltpu.SemaphoreType.DMA((5,)),
            pltpu.SemaphoreType.DMA((5,)),
            pltpu.SemaphoreType.DMA((3,)),
        ],
        compiler_params=pltpu.CompilerParams(
            collective_id=0, has_side_effects=True, vmem_limit_bytes=32 * 1024 * 1024
        ),
    )(
        eigen.reshape(128, 256),
        seg_vec.reshape(6, 16, LANES),
        seg_off.reshape(3, 16, LANES),
        seg_cell.reshape(16, LANES),
        blk_count.reshape(16),
        pair_list.reshape(16, 8).T,
        tab,
    )
    return stress.reshape(8, 16, 256), force.reshape(3, 1, 1, 2048)


def solution(mesh):
    return jax.shard_map(
        functools.partial(per_device, mesh.shape["gx"], mesh.shape["gy"]),
        mesh=mesh,
        in_specs=(
            P("gx", "gy", None),
            P(None, "gx", "gy", None),
            P(None, "gx", "gy", None),
            P("gx", "gy", None),
            P("gx", "gy", None),
            P("gx", "gy", None, None),
        ),
        out_specs=(P("gx", "gy", None), P(None, "gx", "gy", None)),
        check_vma=False,
    )
```

profile of v0, /device:TPU:1, one launch (start us, length us, event | category | flops | bytes accessed | tf_op | source)
XLA Modules:
  0.0 77.7 jit_solution(12336405897629893491)
XLA Ops:
  0.6 0.0 copy-start.4
  0.6 0.0 copy-start.6
  0.7 0.7 copy-done.4
  1.3 0.0 copy-done.6
  1.3 0.0 copy-start
  1.3 0.9 %copy-done = bf16[2,256,256]{2,1,0:T(8,128)(2,1)S(1)} copy-done((bf16[2,256,256]{2,1,0:T(8,128)(2,1)S(1)}, bf16[2,256,256]{2,1,0:T(8,128)(2,1)}, u32[]{:S(2)}) %copy-start) | copy-done | bytes 262168
  2.3 0.0 copy-start.1
  2.3 0.9 %copy-done.1 = f32[8,16,256]{2,1,0:T(8,128)S(1)} copy-done((f32[8,16,256]{2,1,0:T(8,128)S(1)}, f32[8,16,256]{2,1,0:T(8,128)}, u32[]{:S(2)}) %copy-start.1) | copy-done | bytes 131096
  3.2 0.0 copy-start.2
  3.2 0.8 %copy-done.2 = f32[6,1,1,2048]{3,2,1,0:T(1,128)S(1)} copy-done((f32[6,1,1,2048]{3,2,1,0:T(1,128)S(1)}, f32[6,1,1,2048]{3,2,1,0:T(1,128)}, u32[]{:S(2)}) %copy-start.2) | copy-done | bytes 49176
  4.0 0.0 copy-start.3
  4.0 0.7 copy-done.3
  4.7 0.0 copy-start.5
  4.7 0.7 copy-done.5
  5.4 71.0 %shard_map.86 = (f32[128,256]{1,0:T(8,128)S(1)}, f32[3,16,128]{2,1,0:T(8,128)S(1)}) custom-call(f32[128,256]{1,0:T(8,128)S(1)} %bitcast.10, f32[6,16,128]{2,1,0:T(8,128)S(1)} %bitcast.12, f32[3,16,128]{2,1,0:T(8,128)S(1)} %bitcast.13, s32[16,128]{1,0:T(8,128)S(1)} %bitcast.15, s32[16]{0:T(128)S(1)} %bitcast.17, s32[8,16]{1,0:T(8,128)S(1)} %bitcast.16, ...), custom_call_target="tpu_custom_call" | custom-call | tf_op jit(solution)/shard_map/pallas_call | solution.py:344
  76.5 0.7 copy.13
  77.1 0.6 copy.14
Async XLA Ops:
  0.6 0.7 copy-start.4
  0.6 0.7 copy-start.6
  1.3 1.0 %copy-start = (bf16[2,256,256]{2,1,0:T(8,128)(2,1)S(1)}, bf16[2,256,256]{2,1,0:T(8,128)(2,1)}, u32[]{:S(2)}) copy-start(bf16[2,256,256]{2,1,0:T(8,128)(2,1)} %constant.2.clone.tab_hbm) | copy-start | bytes 786436
  2.3 0.9 %copy-start.1 = (f32[8,16,256]{2,1,0:T(8,128)S(1)}, f32[8,16,256]{2,1,0:T(8,128)}, u32[]{:S(2)}) copy-start(f32[8,16,256]{2,1,0:T(8,128)} %param.7) | copy-start | bytes 393220
  3.2 0.8 %copy-start.2 = (f32[6,1,1,2048]{3,2,1,0:T(1,128)S(1)}, f32[6,1,1,2048]{3,2,1,0:T(1,128)}, u32[]{:S(2)}) copy-start(f32[6,1,1,2048]{3,2,1,0:T(1,128)} %param.8) | copy-start | bytes 147460
  4.0 0.7 copy-start.3
  4.7 0.7 copy-start.5
where the time goes:
time: 78.1 us; the launch traced here: 77.7 us
  Pallas kernels  71 us (91%)
  local copies, waits for them, and re-layouts  6.02 us (8%)
    pallas_call x1, Pallas kernels, per_device(): pl.pallas_call(functools.partial(kernel, nx, ny), out_shape=(jax.ShapeDty...  71 us
    unnamed x16, local copies, waits for them, and re-layouts  6.02 us

commit v1 on v0

--- a/solution.py
+++ b/solution.py
@@ -66,10 +66,10 @@
 
 
 def kernel(
-    nx, ny, eigen_hbm, vec_hbm, off_hbm, cell_hbm, count_ref, pair_ref, tab_hbm,
+    nx, ny, eigen_hbm, vec_hbm, off_hbm, cell_hbm, count_hbm, pair_hbm, tab_hbm,
     stress_hbm, force_hbm,
-    eigen, vec, off, cell, tab, send1, recv1, send2, recv2, send3, recv3, send4, recv4,
-    mid_a, mid_b, gain, source, pool, by_block, own_wide, far_wide, pull, hot, stress, force,
+    eigen, vec, off, cell, count_ref, pair_ref, tab, send1, recv1, send2, recv2, send3, recv3, send4, recv4,
+    mid_a, mid_b, gain, source, pool, by_block, own_wide, far_wide, sums, pull, hot, stress, force,
     load_sem, send_sem, recv_sem, store_sem,
 ):
     me_x = lax.axis_index("gx")
@@ -102,6 +102,8 @@
                 (vec_hbm, vec),
                 (off_hbm, off),
                 (cell_hbm, cell),
+                (count_hbm, count_ref),
+                (pair_hbm, pair_ref),
             )
         )
     ]
@@ -125,16 +127,23 @@
 
     pl.semaphore_wait(barrier, nx - 1 + ny - 1 + 4)
 
+    def swing(k, middle):
+        return middle + ((k + 1) >> 1) * (1 - 2 * (k & 1))
+
     def exchange(axis, me, count, send, recv, stage):
+        inner = count // 8
+        outer_me, inner_me = lax.div(me, inner), lax.rem(me, inner)
+
         def push(i, _):
-            peer = lax.rem(me + i, count)
+            outer = lax.rem(outer_me + swing(lax.div(i, inner), 4), 8)
+            peer = outer * inner + lax.rem(inner_me + swing(lax.rem(i, inner), inner // 2), inner)
             pltpu.make_async_remote_copy(
                 src_ref=send.at[peer], dst_ref=recv.at[me], send_sem=send_sem.at[stage],
                 recv_sem=recv_sem.at[stage], device_id={axis: peer}, device_id_type=MESH,
             ).start()
             return 0
 
-        lax.fori_loop(1, count, push, 0)
+        lax.fori_loop(0, count - 1, push, 0)
         recv[me] = send[me]
 
     def arrived(buffer, count, stage):
@@ -153,7 +162,7 @@
     lane_id = lax.broadcasted_iota(jnp.int32, (16, LANES), 1)
     counts = jnp.zeros((16, LANES), jnp.int32)
     for b in range(16):
-        counts = jnp.where(row_id == b, count_ref[b], counts)
+        counts = jnp.where(row_id == b, count_ref[0, b], counts)
     live = jnp.where(lane_id < counts, 1.0, 0.0)
     place = cell[...]
     spots = (place >> 12, (place >> 8) & 15, place & 255)
@@ -178,6 +187,14 @@
         for b in range(16):
             by_block[b, pl.ds(r, 1), :] = rows[b : b + 1]
 
+    def widen(b, _):
+        columns = by_block[b].T
+        for r in range(ROWS):
+            own_wide[b, r] = jnp.broadcast_to(columns[:, r : r + 1], (LANES, LANES))
+        return 0
+
+    lax.fori_loop(0, 16, widen, 0)
+
     def wave(index):
         sine = 2.0 * jnp.sin(index.astype(jnp.float32) * (math.pi / 256.0))
         return sine * sine
@@ -235,13 +252,10 @@
             slot = partner & 15
             for r in range(ROWS):
                 far_wide[n, r] = jnp.broadcast_to(pool[device, r, pl.ds(slot, 1), :], (8, LANES))
-        columns = by_block[b].T
-        for r in range(ROWS):
-            own_wide[r] = jnp.broadcast_to(columns[:, r : r + 1], (LANES, LANES))
 
         def tile(i, _):
             rows = pl.ds(pl.multiple_of(i * 8, 8), 8)
-            own = [own_wide[r, rows, :] for r in range(ROWS)]
+            own = [own_wide[b, r, rows, :] for r in range(ROWS)]
             triple = [3.0 * own[3 + k] for k in range(3)]
             total = [jnp.zeros((8, LANES), jnp.float32) for _ in range(3)]
             for n in range(8):
@@ -257,14 +271,16 @@
                 burg_far = far[3] * delta[0] + far[4] * delta[1] + far[5] * delta[2]
                 weight = (line_dot * inv_three) * (burg_dot - (burg_own * burg_far) * inv_two)
                 total = [total[k] + weight * delta[k] for k in range(3)]
-            lane = lax.broadcasted_iota(jnp.int32, (8, LANES), 1)
-            have = pull[rows, :]
             for k in range(3):
-                have = jnp.where(lane == k * 16 + b, jnp.sum(total[k], axis=1, keepdims=True), have)
-            pull[rows, :] = have
+                sums[k, rows, :] = total[k]
             return 0
 
         lax.fori_loop(0, 16, tile, 0)
+        lane = lax.broadcasted_iota(jnp.int32, (LANES, LANES), 1)
+        have = pull[...]
+        for k in range(3):
+            have = jnp.where(lane == k * 16 + b, jnp.sum(sums[k], axis=1, keepdims=True), have)
+        pull[...] = have
         return 0
 
     pull[...] = jnp.zeros_like(pull)
@@ -339,7 +355,6 @@
     f32, bf16 = jnp.float32, jnp.bfloat16
     tab = jnp.asarray(cas_table(256))
     hbm = pl.BlockSpec(memory_space=pl.ANY)
-    smem = pl.BlockSpec(memory_space=pltpu.SMEM)
     vmem = pltpu.VMEM
     stress, force = pl.pallas_call(
         functools.partial(kernel, nx, ny),
@@ -347,13 +362,15 @@
             jax.ShapeDtypeStruct((128, 256), f32),
             jax.ShapeDtypeStruct((3, 16, LANES), f32),
         ),
-        in_specs=[hbm, hbm, hbm, hbm, smem, smem, hbm],
+        in_specs=[hbm] * 7,
         out_specs=(hbm, hbm),
         scratch_shapes=[
             vmem((2, 128, LANES), f32),
             vmem((6, 16, LANES), f32),
             vmem((3, 16, LANES), f32),
             vmem((16, LANES), jnp.int32),
+            pltpu.SMEM((1, 16), jnp.int32),
+            pltpu.SMEM((8, 16), jnp.int32),
             vmem((2, 256, 256), bf16),
             vmem((32, 8, LANES), f32),
             vmem((32, 8, LANES), f32),
@@ -369,26 +386,27 @@
             vmem((ROWS, 16, LANES), f32),
             vmem((9, ROWS, 16, LANES), f32),
             vmem((16, 16, LANES), f32),
-            vmem((ROWS, LANES, LANES), f32),
+            vmem((16, ROWS, LANES, LANES), f32),
             vmem((8, ROWS, 8, LANES), f32),
+            vmem((3, LANES, LANES), f32),
             vmem((LANES, LANES), f32),
             vmem((256, 2048), bf16),
             vmem((2, 128, LANES), f32),
             vmem((3, 16, LANES), f32),
-            pltpu.SemaphoreType.DMA((6,)),
+            pltpu.SemaphoreType.DMA((8,)),
             pltpu.SemaphoreType.DMA((5,)),
             pltpu.SemaphoreType.DMA((5,)),
             pltpu.SemaphoreType.DMA((3,)),
         ],
         compiler_params=pltpu.CompilerParams(
-            collective_id=0, has_side_effects=True, vmem_limit_bytes=32 * 1024 * 1024
+            collective_id=0, has_side_effects=True, vmem_limit_bytes=60 * 1024 * 1024
         ),
     )(
         eigen.reshape(128, 256),
         seg_vec.reshape(6, 16, LANES),
         seg_off.reshape(3, 16, LANES),
         seg_cell.reshape(16, LANES),
-        blk_count.reshape(16),
+        blk_count.reshape(1, 16),
         pair_list.reshape(16, 8).T,
         tab,
     )

time: 78.1 us -> 51.4 us (0.66)
  Pallas kernels: 71 us -> 48.4 us
  local copies, waits for them, and re-layouts: 6.02 us -> 2.19 us
    pallas_call x1, Pallas kernels: 71 us -> 48.4 us  [per_device(): pl.pallas_call(functools.partial(kernel, nx, ny), out_shape=(jax.ShapeDty...]
    unnamed x16 -> x4, local copies, waits for them, and re-layouts: 6.02 us -> 2.19 us
where the time goes in v1:
time: 51.4 us; the launch traced here: 51.3 us
  Pallas kernels  48.4 us (94%)
  local copies, waits for them, and re-layouts  2.19 us (4%)
  between operations  0.65 us (1%)
    pallas_call x1, Pallas kernels, per_device(): pl.pallas_call(functools.partial(kernel, nx, ny), out_shape=(jax.ShapeDty...  48.4 us
    unnamed x4, local copies, waits for them, and re-layouts  2.19 us

profile of v1, /device:TPU:1, one launch (start us, length us, event | category | flops | bytes accessed | tf_op | source)
XLA Modules:
  0.0 51.3 jit_solution(13968849559097517209)
XLA Ops:
  0.6 48.4 %shard_map.86 = (f32[128,256]{1,0:T(8,128)}, f32[3,16,128]{2,1,0:T(8,128)}) custom-call(f32[128,256]{1,0:T(8,128)} %bitcast.10, f32[6,16,128]{2,1,0:T(8,128)} %bitcast.12, f32[3,16,128]{2,1,0:T(8,128)} %bitcast.13, s32[16,128]{1,0:T(8,128)} %bitcast.15, s32[1,16]{1,0:T(1,128)} %bitcast.17, s32[8,16]{1,0:T(8,128)} %bitcast.16, ...), custom_call_target="tpu_custom_call" | custom-call | tf_op jit(solution)/shard_map/pallas_call | solution.py:359
  49.1 0.0 copy-start
  49.1 1.6 %copy.13 = f32[8,16,256]{2,1,0:T(8,128)} copy(f32[8,16,256]{2,1,0:T(8,128)} %bitcast.11) | data formatting | bytes 262144
  50.7 0.0 copy-done
  50.7 0.6 %copy.14 = f32[3,1,1,2048]{3,2,1,0:T(1,128)} copy(f32[3,1,1,2048]{3,2,1,0:T(1,128)S(1)} %bitcast.14) | data formatting | bytes 49152
Async XLA Ops:
  49.1 1.6 %copy-start = (f32[3,16,128]{2,1,0:T(8,128)S(1)}, f32[3,16,128]{2,1,0:T(8,128)}, u32[]{:S(2)}) copy-start(f32[3,16,128]{2,1,0:T(8,128)} %get-tuple-element.5) | copy-start | bytes 73732

commit v2 on v1

--- a/solution.py
+++ b/solution.py
@@ -17,6 +17,7 @@
 MESH = pl.DeviceIdType.MESH
 ROWS = 9
 LANES = 128
+CUT = (5, 10)
 
 
 def cas_table(length):
@@ -31,6 +32,12 @@
 def parts(x):
     high = x.astype(jnp.bfloat16)
     return high, (x - high.astype(jnp.float32)).astype(jnp.bfloat16)
+
+
+def three_parts(x):
+    high = x.astype(jnp.bfloat16)
+    rest = x - high.astype(jnp.float32)
+    return high, *parts(rest)
 
 
 def mm(a, b):
@@ -66,31 +73,22 @@
 
 
 def kernel(
-    nx, ny, eigen_hbm, vec_hbm, off_hbm, cell_hbm, count_hbm, pair_hbm, tab_hbm,
-    stress_hbm, force_hbm,
-    eigen, vec, off, cell, count_ref, pair_ref, tab, send1, recv1, send2, recv2, send3, recv3, send4, recv4,
-    mid_a, mid_b, gain, source, pool, by_block, own_wide, far_wide, sums, pull, hot, stress, force,
-    load_sem, send_sem, recv_sem, store_sem,
+    nx, ny, eigen_hbm, vec_hbm, off_hbm, cell_hbm, count_hbm, pair_hbm, tab_hbm, wave_hbm,
+    stress, force,
+    eigen, vec, off, cell, count_ref, pair_ref, tab, wave, send1, recv1, send2, recv2, send3, recv3, send4, recv4,
+    mid_a, mid_b, gain, source, pool, by_block, own_wide, far_wide, sums, pull, hot,
+    load_sem, send_sem, recv_sem,
 ):
     me_x = lax.axis_index("gx")
     me_y = lax.axis_index("gy")
 
-    barrier = pltpu.get_barrier_semaphore()
-
-    def greet_x(i, _):
-        pl.semaphore_signal(barrier, inc=1, device_id={"gx": lax.rem(me_x + i, nx)}, device_id_type=MESH)
-        return 0
-
-    def greet_y(i, _):
-        pl.semaphore_signal(barrier, inc=1, device_id={"gy": lax.rem(me_y + i, ny)}, device_id_type=MESH)
-        return 0
-
-    lax.fori_loop(1, nx, greet_x, 0)
-    lax.fori_loop(1, ny, greet_y, 0)
-    for dx in (-1, 1):
-        for dy in (-1, 1):
-            peer = {"gx": lax.rem(me_x + dx + nx, nx), "gy": lax.rem(me_y + dy + ny, ny)}
-            pl.semaphore_signal(barrier, inc=1, device_id=peer, device_id_type=MESH)
+    def swing(k, middle):
+        return middle + ((k + 1) >> 1) * (1 - 2 * (k & 1))
+
+    def peer_of(me, count, i):
+        inner = count // 8
+        outer = ((me // inner) + swing(i // inner, 4)) & 7
+        return outer * inner + ((me + swing(i % inner, inner // 2)) & (inner - 1))
 
     loads = [
         pltpu.make_async_copy(src, dst, load_sem.at[n])
@@ -104,11 +102,21 @@
                 (cell_hbm, cell),
                 (count_hbm, count_ref),
                 (pair_hbm, pair_ref),
+                (wave_hbm, wave),
             )
         )
     ]
     for load in loads:
         load.start()
+
+    barrier = pltpu.get_barrier_semaphore()
+
+    for axis, me, count in (("gx", me_x, nx), ("gy", me_y, ny)):
+        for i in range(count - 1):
+            pl.semaphore_signal(
+                barrier, inc=1, device_id={axis: peer_of(me, count, i)}, device_id_type=MESH
+            )
+
     for load in loads[:3]:
         load.wait()
 
@@ -125,25 +133,15 @@
         for j, tile in enumerate(swap_blocks(tiles, 8)):
             send1[h * 16 + j] = tile
 
-    pl.semaphore_wait(barrier, nx - 1 + ny - 1 + 4)
-
-    def swing(k, middle):
-        return middle + ((k + 1) >> 1) * (1 - 2 * (k & 1))
+    pl.semaphore_wait(barrier, nx - 1 + ny - 1)
 
     def exchange(axis, me, count, send, recv, stage):
-        inner = count // 8
-        outer_me, inner_me = lax.div(me, inner), lax.rem(me, inner)
-
-        def push(i, _):
-            outer = lax.rem(outer_me + swing(lax.div(i, inner), 4), 8)
-            peer = outer * inner + lax.rem(inner_me + swing(lax.rem(i, inner), inner // 2), inner)
+        for i in range(count - 1):
+            peer = peer_of(me, count, i)
             pltpu.make_async_remote_copy(
                 src_ref=send.at[peer], dst_ref=recv.at[me], send_sem=send_sem.at[stage],
                 recv_sem=recv_sem.at[stage], device_id={axis: peer}, device_id_type=MESH,
             ).start()
-            return 0
-
-        lax.fori_loop(0, count - 1, push, 0)
         recv[me] = send[me]
 
     def arrived(buffer, count, stage):
@@ -170,54 +168,62 @@
         source[k] = spots[k].astype(jnp.float32) + off[k]
         source[3 + k] = vec[k] * live
         source[6 + k] = vec[3 + k]
-    for dx in (-1, 0, 1):
-        for dy in (-1, 0, 1):
-            if dx == 0 and dy == 0:
-                continue
-            peer = {"gx": lax.rem(me_x + dx + nx, nx), "gy": lax.rem(me_y + dy + ny, ny)}
-            pltpu.make_async_remote_copy(
-                src_ref=source, dst_ref=pool.at[(1 - dx) * 3 + (1 - dy)], send_sem=send_sem.at[4],
-                recv_sem=recv_sem.at[4], device_id=peer, device_id_type=MESH,
-            ).start()
+
+    def pass_on(column, p, q, axis, me, count, step, stage):
+        pltpu.make_async_remote_copy(
+            src_ref=column, dst_ref=pool.at[p * 3 + q], send_sem=send_sem.at[4], recv_sem=recv_sem.at[stage],
+            device_id={axis: (me + step) & (count - 1)}, device_id_type=MESH,
+        ).start()
+
+    for step in (-1, 1):
+        pass_on(source, 1 - step, 1, "gx", me_x, nx, step, 4)
+    for step in (-1, 1):
+        pass_on(source, 1, 1 - step, "gy", me_y, ny, step, 5)
     for r in range(ROWS):
         pool[4, r] = source[r]
 
+    by_block[...] = jnp.zeros_like(by_block)
     for r in range(ROWS):
         rows = source[r]
         for b in range(16):
             by_block[b, pl.ds(r, 1), :] = rows[b : b + 1]
 
+    row = lax.broadcasted_iota(jnp.int32, (48, ROWS * LANES), 0) & 15
+    spread = jnp.where(row == lax.broadcasted_iota(jnp.int32, (48, ROWS * LANES), 1) >> 7, 1.0, 0.0)
+    spread = spread.astype(jnp.bfloat16)
+
     def widen(b, _):
-        columns = by_block[b].T
+        rows = jnp.concatenate([part.astype(jnp.float32) for part in three_parts(by_block[b])], axis=0)
+        wide = mm(rows.T.astype(jnp.bfloat16), spread)
         for r in range(ROWS):
-            own_wide[b, r] = jnp.broadcast_to(columns[:, r : r + 1], (LANES, LANES))
+            own_wide[b, r] = wide[:, r * LANES : (r + 1) * LANES]
         return 0
 
-    lax.fori_loop(0, 16, widen, 0)
-
-    def wave(index):
+    lax.fori_loop(0, 16, widen, 0, unroll=4)
+
+    arrived(pool, 2, 4)
+    for step in (-1, 1):
+        for p in (0, 2):
+            pass_on(pool.at[p * 3 + 1], p, 1 - step, "gy", me_y, ny, step, 5)
+
+    lane = lax.broadcasted_iota(jnp.int32, (8, LANES), 1)
+    freq_z = me_x * 8 + (lane >> 4)
+    freq_x = me_y * 16 + (lane & 15)
+
+    def wave_of(index):
         sine = 2.0 * jnp.sin(index.astype(jnp.float32) * (math.pi / 256.0))
         return sine * sine
 
-    lane_row = lax.broadcasted_iota(jnp.int32, (8, LANES), 1)
-    freq_z = me_x * 8 + (lane_row >> 4)
-    freq_x = me_y * 16 + (lane_row & 15)
-    wave_x, wave_z = wave(freq_x), wave(freq_z)
+    wave_x, wave_z = wave_of(freq_x), wave_of(freq_z)
     both = wave_x + wave_z
     product = 2.0 / (1.0 - nu_copper) * wave_x * wave_z
     corner = (freq_x == 0) & (freq_z == 0)
-
-    def fill_gain(i, _):
-        freq_y = i * 8 + lax.broadcasted_iota(jnp.int32, (8, LANES), 0)
-        total = both + wave(freq_y)
-        safe = jnp.where(corner & (freq_y == 0), 1.0, total)
-        inverse = 1.0 / safe
-        gain[pl.ds(pl.multiple_of(i * 8, 8), 8), :] = (-2.0 / 256.0**3) * (
-            1.0 - both * inverse + product * inverse * inverse
-        )
-        return 0
-
-    lax.fori_loop(0, 32, fill_gain, 0)
+    for i in range(32):
+        total = both + wave[pl.ds(i * 8, 8), :]
+        if i == 0:
+            total = jnp.where(corner & (lax.broadcasted_iota(jnp.int32, (8, LANES), 0) == 0), 1.0, total)
+        inverse = 1.0 / total
+        gain[pl.ds(i * 8, 8), :] = (-2.0 / 256.0**3) * (1.0 - both * inverse + product * inverse * inverse)
 
     spot = ((place >> 7) & 1) * 128 + ((place >> 8) & 15) * 8 + (place >> 12)
     for b in range(16):
@@ -225,33 +231,17 @@
         at = lax.broadcasted_iota(jnp.int32, (256, LANES), 0)
         hot[:, b * LANES : (b + 1) * LANES] = jnp.where(want == at, 1.0, 0.0).astype(jnp.bfloat16)
 
-    arrived(recv1, nx - 1, 0)
-    held = recv1[...].reshape(256, LANES)
-    along_x = times_table(held.T, tab)
-    for h in range(2):
-        mid_a[h] = along_x[:, h * LANES : (h + 1) * LANES]
-    for h in range(2):
-        for s in range(2):
-            tiles = [mid_a[h, pl.ds(s * 64 + c, 8, stride=8), :] for c in range(8)]
-            for j, tile in enumerate(swap_blocks(tiles, 16)):
-                send2[h * 8 + j, s * 8 : s * 8 + 8, :] = tile
-    exchange("gy", me_y, ny, send2, recv2, 1)
-
-    arrived(pool, 8, 4)
-    for p in range(3):
-        for q in range(3):
-            if p != 1:
-                pool[p * 3 + q, 0] += (p - 1) * 8.0
-            if q != 1:
-                pool[p * 3 + q, 1] += (q - 1) * 16.0
-
     def pair_block(b, _):
         for n in range(8):
             partner = pair_ref[n, b]
             device = partner >> 4
             slot = partner & 15
+            shift = {0: (lax.div(device, 3) - 1) * 8, 1: (lax.rem(device, 3) - 1) * 16}
             for r in range(ROWS):
-                far_wide[n, r] = jnp.broadcast_to(pool[device, r, pl.ds(slot, 1), :], (8, LANES))
+                far = pool[device, r, pl.ds(slot, 1), :]
+                if r in shift:
+                    far = far + shift[r].astype(jnp.float32)
+                far_wide[n, r] = jnp.broadcast_to(far, (8, LANES))
 
         def tile(i, _):
             rows = pl.ds(pl.multiple_of(i * 8, 8), 8)
@@ -272,25 +262,44 @@
                 weight = (line_dot * inv_three) * (burg_dot - (burg_own * burg_far) * inv_two)
                 total = [total[k] + weight * delta[k] for k in range(3)]
             for k in range(3):
-                sums[k, rows, :] = total[k]
+                sums[b, k, rows, :] = total[k]
             return 0
 
         lax.fori_loop(0, 16, tile, 0)
-        lane = lax.broadcasted_iota(jnp.int32, (LANES, LANES), 1)
+        return 0
+
+    def pair_blocks(first, end):
+        lax.fori_loop(first, end, pair_block, 0)
+        column = lax.broadcasted_iota(jnp.int32, (2 * LANES, LANES), 1)
         have = pull[...]
-        for k in range(3):
-            have = jnp.where(lane == k * 16 + b, jnp.sum(sums[k], axis=1, keepdims=True), have)
+        for b in range(first, end):
+            for k in range(3):
+                pick = jnp.where(column == k * 16 + b, 1.0, 0.0).astype(jnp.bfloat16)
+                have = have + mm(jnp.concatenate(parts(sums[b, k]), axis=1), pick)
         pull[...] = have
-        return 0
 
     pull[...] = jnp.zeros_like(pull)
-    lax.fori_loop(0, 5, pair_block, 0)
+
+    arrived(recv1, nx - 1, 0)
+    held = recv1[...].reshape(256, LANES)
+    along_x = times_table(held.T, tab)
+    for h in range(2):
+        mid_a[h] = along_x[:, h * LANES : (h + 1) * LANES]
+    for h in range(2):
+        for s in range(2):
+            tiles = [mid_a[h, pl.ds(s * 64 + c, 8, stride=8), :] for c in range(8)]
+            for j, tile in enumerate(swap_blocks(tiles, 16)):
+                send2[h * 8 + j, s * 8 : s * 8 + 8, :] = tile
+    exchange("gy", me_y, ny, send2, recv2, 1)
+
+    arrived(pool, 6, 5)
+    pair_blocks(0, CUT[0])
 
     arrived(recv2, ny - 1, 1)
     spectrum = table_times(tab, recv2[...].reshape(256, LANES)) * gain[...]
     send3[...] = table_times(tab, spectrum).reshape(16, 16, LANES)
     exchange("gy", me_y, ny, send3, recv3, 2)
-    lax.fori_loop(5, 10, pair_block, 0)
+    pair_blocks(CUT[0], CUT[1])
 
     arrived(recv3, ny - 1, 2)
     for h in range(2):
@@ -301,7 +310,7 @@
     back_x = jnp.concatenate([mid_b[0], mid_b[1]], axis=1).T
     send4[...] = table_times(tab, back_x).reshape(32, 8, LANES)
     exchange("gx", me_x, nx, send4, recv4, 3)
-    lax.fori_loop(10, 16, pair_block, 0)
+    pair_blocks(CUT[1], 16)
 
     arrived(recv4, nx - 1, 3)
     halves = []
@@ -311,16 +320,7 @@
     final = times_table(jnp.concatenate(halves, axis=1), tab)
     for h in range(2):
         for y in range(16):
-            stress[h, pl.ds(y, 8, stride=16), :] = final[y * 8 : y * 8 + 8, h * LANES : (h + 1) * LANES]
-    stores = [
-        pltpu.make_async_copy(
-            stress.at[h], stress_hbm.at[:, pl.ds(h * LANES, LANES)], store_sem.at[h]
-        )
-        for h in range(2)
-    ]
-    for store in stores:
-        store.start()
-
+            stress[pl.ds(h * 128 + y, 8, stride=16), :] = final[y * 8 : y * 8 + 8, h * LANES : (h + 1) * LANES]
     tall = jnp.concatenate([final[:, :LANES], final[:, LANES:]], axis=0).T
     high, low = parts(tall)
     depth = place & 127
@@ -339,31 +339,29 @@
         k1, k2 = (k + 1) % 3, (k + 2) % 3
         glide = burgers[k1] * tangent[k2] - burgers[k2] * tangent[k1]
         force[k] = pair_scale * pulled[k * 16 : k * 16 + 16] + tau * glide
-    last = pltpu.make_async_copy(force, force_hbm, store_sem.at[2])
-    last.start()
     left(send1, nx - 1, 0)
     left(send2, ny - 1, 1)
     left(send3, ny - 1, 2)
     left(send4, nx - 1, 3)
     left(pool, 8, 4)
-    for store in stores:
-        store.wait()
-    last.wait()
 
 
 def per_device(nx, ny, eigen, seg_vec, seg_off, seg_cell, blk_count, pair_list):
     f32, bf16 = jnp.float32, jnp.bfloat16
     tab = jnp.asarray(cas_table(256))
-    hbm = pl.BlockSpec(memory_space=pl.ANY)
+    sines = 2.0 * np.sin(np.arange(256) * (math.pi / 256.0))
+    wave = jnp.asarray(np.repeat((sines * sines).astype(np.float32)[:, None], LANES, axis=1))
+    hbm = pl.BlockSpec(memory_space=pltpu.HBM)
+    out = pl.BlockSpec(memory_space=pltpu.VMEM)
     vmem = pltpu.VMEM
     stress, force = pl.pallas_call(
         functools.partial(kernel, nx, ny),
         out_shape=(
-            jax.ShapeDtypeStruct((128, 256), f32),
-            jax.ShapeDtypeStruct((3, 16, LANES), f32),
+            vmem((256, LANES), f32),
+            vmem((3, 16, LANES), f32),
         ),
-        in_specs=[hbm] * 7,
-        out_specs=(hbm, hbm),
+        in_specs=[hbm] * 8,
+        out_specs=(out, out),
         scratch_shapes=[
             vmem((2, 128, LANES), f32),
             vmem((6, 16, LANES), f32),
@@ -372,6 +370,7 @@
             pltpu.SMEM((1, 16), jnp.int32),
             pltpu.SMEM((8, 16), jnp.int32),
             vmem((2, 256, 256), bf16),
+            vmem((256, LANES), f32),
             vmem((32, 8, LANES), f32),
             vmem((32, 8, LANES), f32),
             vmem((16, 16, LANES), f32),
@@ -388,15 +387,12 @@
             vmem((16, 16, LANES), f32),
             vmem((16, ROWS, LANES, LANES), f32),
             vmem((8, ROWS, 8, LANES), f32),
-            vmem((3, LANES, LANES), f32),
+            vmem((16, 3, LANES, LANES), f32),
             vmem((LANES, LANES), f32),
             vmem((256, 2048), bf16),
-            vmem((2, 128, LANES), f32),
-            vmem((3, 16, LANES), f32),
-            pltpu.SemaphoreType.DMA((8,)),
+            pltpu.SemaphoreType.DMA((9,)),
             pltpu.SemaphoreType.DMA((5,)),
-            pltpu.SemaphoreType.DMA((5,)),
-            pltpu.SemaphoreType.DMA((3,)),
+            pltpu.SemaphoreType.DMA((6,)),
         ],
         compiler_params=pltpu.CompilerParams(
             collective_id=0, has_side_effects=True, vmem_limit_bytes=60 * 1024 * 1024
@@ -409,7 +405,9 @@
         blk_count.reshape(1, 16),
         pair_list.reshape(16, 8).T,
         tab,
+        wave,
     )
+    stress = jnp.concatenate([stress[:128], stress[128:]], axis=1)
     return stress.reshape(8, 16, 256), force.reshape(3, 1, 1, 2048)
 
 

time: 51.4 us -> 51.1 us (level)
  local copies, waits for them, and re-layouts: 2.19 us -> 0.62 us
  other arithmetic: 0 us -> 0.67 us
  Pallas kernels: 48.4 us -> 49 us
    unnamed x4 -> x1, local copies, waits for them, and re-layouts: 2.19 us -> 0.61 us
    concatenate x0 -> x1, other arithmetic: none -> 0.67 us  [per_device(): stress = jnp.concatenate([stress[:128], stress[128:]], axis=1)]
    pallas_call x1, Pallas kernels: 48.4 us -> 49 us  [per_device(): pl.pallas_call(functools.partial(kernel, nx, ny), out_shape=(vmem((256, L...]
where the time goes in v2:
time: 51.1 us; the launch traced here: 51 us
  Pallas kernels  49 us (96%)
  other arithmetic  0.67 us (1%)
  between operations  0.64 us (1%)
  local copies, waits for them, and re-layouts  0.62 us (1%)
    pallas_call x1, Pallas kernels, per_device(): pl.pallas_call(functools.partial(kernel, nx, ny), out_shape=(vmem((256, L...  49 us

profile of v2, /device:TPU:1, one launch (start us, length us, event | category | flops | bytes accessed | tf_op | source)
XLA Modules:
  0.0 51.0 jit_solution(2793864205445206777)
XLA Ops:
  0.6 49.0 %shard_map.95 = (f32[256,128]{1,0:T(8,128)S(1)}, f32[3,16,128]{2,1,0:T(8,128)S(1)}) custom-call(f32[128,256]{1,0:T(8,128)} %bitcast.12, f32[6,16,128]{2,1,0:T(8,128)} %bitcast.13, f32[3,16,128]{2,1,0:T(8,128)} %bitcast.14, s32[16,128]{1,0:T(8,128)} %bitcast.15, s32[1,16]{1,0:T(1,128)} %bitcast.17, s32[8,16]{1,0:T(8,128)} %bitcast.16, ...), custom_call_target="tpu_custom_call" | custom-call | tf_op jit(solution)/shard_map/pallas_call | solution.py:357
  49.7 0.6 %copy.13 = f32[3,1,1,2048]{3,2,1,0:T(1,128)} copy(f32[3,1,1,2048]{3,2,1,0:T(1,128)S(1)} %bitcast.10) | data formatting | bytes 49152
  50.3 0.7 %pad_maximum_fusion = f32[128,256]{1,0:T(8,128)} fusion(f32[128,128]{1,0:T(8,128)S(1)} %get-tuple-element.11, f32[128,128]{1,0:T(8,128)S(1)} %get-tuple-element.10), kind=kLoop, calls=%fused_computation | loop fusion | flops 32768 | bytes 262144 | tf_op jit(solution)/shard_map/concatenate | solution.py:410
  (1 shorter events, 0.0 us)

commit v3 on v2

--- a/solution.py
+++ b/solution.py
@@ -117,43 +117,6 @@
                 barrier, inc=1, device_id={axis: peer_of(me, count, i)}, device_id_type=MESH
             )
 
-    for load in loads[:3]:
-        load.wait()
-
-    lines = jnp.concatenate(
-        [
-            jnp.concatenate([eigen[h, pl.ds(y, 8, stride=16), :] for h in range(2)], axis=1)
-            for y in range(16)
-        ],
-        axis=0,
-    )
-    zeta = times_table(lines, tab)
-    for h in range(2):
-        tiles = [zeta[y * 8 : y * 8 + 8, h * LANES : (h + 1) * LANES] for y in range(16)]
-        for j, tile in enumerate(swap_blocks(tiles, 8)):
-            send1[h * 16 + j] = tile
-
-    pl.semaphore_wait(barrier, nx - 1 + ny - 1)
-
-    def exchange(axis, me, count, send, recv, stage):
-        for i in range(count - 1):
-            peer = peer_of(me, count, i)
-            pltpu.make_async_remote_copy(
-                src_ref=send.at[peer], dst_ref=recv.at[me], send_sem=send_sem.at[stage],
-                recv_sem=recv_sem.at[stage], device_id={axis: peer}, device_id_type=MESH,
-            ).start()
-        recv[me] = send[me]
-
-    def arrived(buffer, count, stage):
-        whole = buffer.at[pl.ds(0, count)]
-        pltpu.make_async_copy(whole, whole, recv_sem.at[stage]).wait()
-
-    def left(buffer, count, stage):
-        whole = buffer.at[pl.ds(0, count)]
-        pltpu.make_async_copy(whole, whole, send_sem.at[stage]).wait()
-
-    exchange("gx", me_x, nx, send1, recv1, 0)
-
     for load in loads[3:]:
         load.wait()
     row_id = lax.broadcasted_iota(jnp.int32, (16, LANES), 0)
@@ -168,6 +131,40 @@
         source[k] = spots[k].astype(jnp.float32) + off[k]
         source[3 + k] = vec[k] * live
         source[6 + k] = vec[3 + k]
+    for load in loads[:3]:
+        load.wait()
+
+    lines = jnp.concatenate(
+        [
+            jnp.concatenate([eigen[h, pl.ds(y, 8, stride=16), :] for h in range(2)], axis=1)
+            for y in range(16)
+        ],
+        axis=0,
+    )
+    zeta = times_table(lines, tab)
+    for h in range(2):
+        tiles = [zeta[y * 8 : y * 8 + 8, h * LANES : (h + 1) * LANES] for y in range(16)]
+        for j, tile in enumerate(swap_blocks(tiles, 8)):
+            send1[h * 16 + j] = tile
+
+    pl.semaphore_wait(barrier, nx - 1 + ny - 1)
+
+    def exchange(axis, me, count, send, recv, stage):
+        for i in range(count - 1):
+            peer = peer_of(me, count, i)
+            pltpu.make_async_remote_copy(
+                src_ref=send.at[peer], dst_ref=recv.at[me], send_sem=send_sem.at[stage],
+                recv_sem=recv_sem.at[stage], device_id={axis: peer}, device_id_type=MESH,
+            ).start()
+        recv[me] = send[me]
+
+    def arrived(buffer, count, stage):
+        whole = buffer.at[pl.ds(0, count)]
+        pltpu.make_async_copy(whole, whole, recv_sem.at[stage]).wait()
+
+    def left(buffer, count, stage):
+        whole = buffer.at[pl.ds(0, count)]
+        pltpu.make_async_copy(whole, whole, send_sem.at[stage]).wait()
 
     def pass_on(column, p, q, axis, me, count, step, stage):
         pltpu.make_async_remote_copy(
@@ -179,6 +176,8 @@
         pass_on(source, 1 - step, 1, "gx", me_x, nx, step, 4)
     for step in (-1, 1):
         pass_on(source, 1, 1 - step, "gy", me_y, ny, step, 5)
+    exchange("gx", me_x, nx, send1, recv1, 0)
+
     for r in range(ROWS):
         pool[4, r] = source[r]
 

time: 51.1 us -> 49.5 us (0.969)
  Pallas kernels: 49 us -> 47.4 us
    pallas_call x1, Pallas kernels: 49 us -> 47.4 us  [per_device(): pl.pallas_call(functools.partial(kernel, nx, ny), out_shape=(vmem((256, L...]
where the time goes in v3:
time: 49.5 us; the launch traced here: 49.3 us
  Pallas kernels  47.4 us (96%)
  other arithmetic  0.67 us (1%)
  between operations  0.64 us (1%)
  local copies, waits for them, and re-layouts  0.62 us (1%)
    pallas_call x1, Pallas kernels, per_device(): pl.pallas_call(functools.partial(kernel, nx, ny), out_shape=(vmem((256, L...  47.4 us

profile of v3, /device:TPU:1, one launch (start us, length us, event | category | flops | bytes accessed | tf_op | source)
XLA Modules:
  0.0 49.3 jit_solution(4483532505600913867)
XLA Ops:
  0.6 47.4 %shard_map.95 = (f32[256,128]{1,0:T(8,128)S(1)}, f32[3,16,128]{2,1,0:T(8,128)S(1)}) custom-call(f32[128,256]{1,0:T(8,128)} %bitcast.12, f32[6,16,128]{2,1,0:T(8,128)} %bitcast.13, f32[3,16,128]{2,1,0:T(8,128)} %bitcast.14, s32[16,128]{1,0:T(8,128)} %bitcast.15, s32[1,16]{1,0:T(1,128)} %bitcast.17, s32[8,16]{1,0:T(8,128)} %bitcast.16, ...), custom_call_target="tpu_custom_call" | custom-call | tf_op jit(solution)/shard_map/pallas_call | solution.py:356
  48.0 0.6 %copy.13 = f32[3,1,1,2048]{3,2,1,0:T(1,128)} copy(f32[3,1,1,2048]{3,2,1,0:T(1,128)S(1)} %bitcast.10) | data formatting | bytes 49152
  48.7 0.7 %pad_maximum_fusion = f32[128,256]{1,0:T(8,128)} fusion(f32[128,128]{1,0:T(8,128)S(1)} %get-tuple-element.11, f32[128,128]{1,0:T(8,128)S(1)} %get-tuple-element.10), kind=kLoop, calls=%fused_computation | loop fusion | flops 32768 | bytes 262144 | tf_op jit(solution)/shard_map/concatenate | solution.py:409
  (1 shorter events, 0.0 us)

commit v4 on v3

--- a/solution.py
+++ b/solution.py
@@ -147,6 +147,25 @@
         for j, tile in enumerate(swap_blocks(tiles, 8)):
             send1[h * 16 + j] = tile
 
+    by_block[...] = jnp.zeros_like(by_block)
+    for r in range(ROWS):
+        rows = source[r]
+        for b in range(16):
+            by_block[b, pl.ds(r, 1), :] = rows[b : b + 1]
+
+    row = lax.broadcasted_iota(jnp.int32, (48, ROWS * LANES), 0) & 15
+    spread = jnp.where(row == lax.broadcasted_iota(jnp.int32, (48, ROWS * LANES), 1) >> 7, 1.0, 0.0)
+    spread = spread.astype(jnp.bfloat16)
+
+    def widen(b, _):
+        rows = jnp.concatenate([part.astype(jnp.float32) for part in three_parts(by_block[b])], axis=0)
+        wide = mm(rows.T.astype(jnp.bfloat16), spread)
+        for r in range(ROWS):
+            own_wide[b, r] = wide[:, r * LANES : (r + 1) * LANES]
+        return 0
+
+    lax.fori_loop(0, 16, widen, 0, unroll=4)
+
     pl.semaphore_wait(barrier, nx - 1 + ny - 1)
 
     def exchange(axis, me, count, send, recv, stage):
@@ -173,37 +192,18 @@
         ).start()
 
     for step in (-1, 1):
-        pass_on(source, 1 - step, 1, "gx", me_x, nx, step, 4)
+        pass_on(source, 1, 1 - step, "gy", me_y, ny, step, 4)
     for step in (-1, 1):
-        pass_on(source, 1, 1 - step, "gy", me_y, ny, step, 5)
+        pass_on(source, 1 - step, 1, "gx", me_x, nx, step, 5)
     exchange("gx", me_x, nx, send1, recv1, 0)
 
     for r in range(ROWS):
         pool[4, r] = source[r]
 
-    by_block[...] = jnp.zeros_like(by_block)
-    for r in range(ROWS):
-        rows = source[r]
-        for b in range(16):
-            by_block[b, pl.ds(r, 1), :] = rows[b : b + 1]
-
-    row = lax.broadcasted_iota(jnp.int32, (48, ROWS * LANES), 0) & 15
-    spread = jnp.where(row == lax.broadcasted_iota(jnp.int32, (48, ROWS * LANES), 1) >> 7, 1.0, 0.0)
-    spread = spread.astype(jnp.bfloat16)
-
-    def widen(b, _):
-        rows = jnp.concatenate([part.astype(jnp.float32) for part in three_parts(by_block[b])], axis=0)
-        wide = mm(rows.T.astype(jnp.bfloat16), spread)
-        for r in range(ROWS):
-            own_wide[b, r] = wide[:, r * LANES : (r + 1) * LANES]
-        return 0
-
-    lax.fori_loop(0, 16, widen, 0, unroll=4)
-
     arrived(pool, 2, 4)
     for step in (-1, 1):
-        for p in (0, 2):
-            pass_on(pool.at[p * 3 + 1], p, 1 - step, "gy", me_y, ny, step, 5)
+        for q in (0, 2):
+            pass_on(pool.at[3 + q], 1 - step, q, "gx", me_x, nx, step, 5)
 
     lane = lax.broadcasted_iota(jnp.int32, (8, LANES), 1)
     freq_z = me_x * 8 + (lane >> 4)
@@ -264,17 +264,19 @@
                 sums[b, k, rows, :] = total[k]
             return 0
 
-        lax.fori_loop(0, 16, tile, 0)
+        lax.fori_loop(0, 16, tile, 0, unroll=4)
         return 0
 
     def pair_blocks(first, end):
         lax.fori_loop(first, end, pair_block, 0)
-        column = lax.broadcasted_iota(jnp.int32, (2 * LANES, LANES), 1)
+        high, low = parts(sums[first:end].reshape((end - first) * 3 * LANES, LANES))
+        ones = jnp.ones((2 * LANES, LANES), jnp.bfloat16)
+        added = mm(jnp.concatenate([high, low], axis=1), ones)
+        column = lax.broadcasted_iota(jnp.int32, (LANES, LANES), 1)
         have = pull[...]
-        for b in range(first, end):
-            for k in range(3):
-                pick = jnp.where(column == k * 16 + b, 1.0, 0.0).astype(jnp.bfloat16)
-                have = have + mm(jnp.concatenate(parts(sums[b, k]), axis=1), pick)
+        for n in range((end - first) * 3):
+            spot = (n % 3) * 16 + first + n // 3
+            have = jnp.where(column == spot, added[n * LANES : (n + 1) * LANES], have)
         pull[...] = have
 
     pull[...] = jnp.zeros_like(pull)

time: 49.5 us -> 48.2 us (0.974)
  Pallas kernels: 47.4 us -> 46.2 us
    pallas_call x1, Pallas kernels: 47.4 us -> 46.2 us  [per_device(): pl.pallas_call(functools.partial(kernel, nx, ny), out_shape=(vmem((256, L...]
where the time goes in v4:
time: 48.2 us; the launch traced here: 48.1 us
  Pallas kernels  46.2 us (96%)
  other arithmetic  0.67 us (1%)
  between operations  0.64 us (1%)
  local copies, waits for them, and re-layouts  0.62 us (1%)
    pallas_call x1, Pallas kernels, per_device(): pl.pallas_call(functools.partial(kernel, nx, ny), out_shape=(vmem((256, L...  46.2 us

profile of v4, /device:TPU:1, one launch (start us, length us, event | category | flops | bytes accessed | tf_op | source)
XLA Modules:
  0.0 48.1 jit_solution(14611444908532651292)
XLA Ops:
  0.6 46.2 %shard_map.95 = (f32[256,128]{1,0:T(8,128)S(1)}, f32[3,16,128]{2,1,0:T(8,128)S(1)}) custom-call(f32[128,256]{1,0:T(8,128)} %bitcast.12, f32[6,16,128]{2,1,0:T(8,128)} %bitcast.13, f32[3,16,128]{2,1,0:T(8,128)} %bitcast.14, s32[16,128]{1,0:T(8,128)} %bitcast.15, s32[1,16]{1,0:T(1,128)} %bitcast.17, s32[8,16]{1,0:T(8,128)} %bitcast.16, ...), custom_call_target="tpu_custom_call" | custom-call | tf_op jit(solution)/shard_map/pallas_call | solution.py:358
  46.8 0.6 %copy.13 = f32[3,1,1,2048]{3,2,1,0:T(1,128)} copy(f32[3,1,1,2048]{3,2,1,0:T(1,128)S(1)} %bitcast.10) | data formatting | bytes 49152
  47.4 0.7 %pad_maximum_fusion = f32[128,256]{1,0:T(8,128)} fusion(f32[128,128]{1,0:T(8,128)S(1)} %get-tuple-element.11, f32[128,128]{1,0:T(8,128)S(1)} %get-tuple-element.10), kind=kLoop, calls=%fused_computation | loop fusion | flops 32768 | bytes 262144 | tf_op jit(solution)/shard_map/concatenate | solution.py:411
  (1 shorter events, 0.0 us)

commit v5 on v4

--- a/solution.py
+++ b/solution.py
@@ -192,7 +192,7 @@
         ).start()
 
     for step in (-1, 1):
-        pass_on(source, 1, 1 - step, "gy", me_y, ny, step, 4)
+        pass_on(source, 1, 1 - step, "gy", me_y, ny, step, 4 + (1 - step))
     for step in (-1, 1):
         pass_on(source, 1 - step, 1, "gx", me_x, nx, step, 5)
     exchange("gx", me_x, nx, send1, recv1, 0)
@@ -200,10 +200,14 @@
     for r in range(ROWS):
         pool[4, r] = source[r]
 
-    arrived(pool, 2, 4)
-    for step in (-1, 1):
-        for q in (0, 2):
+    def relay(q):
+        arrived(pool, 1, 4 + q)
+        for step in (-1, 1):
             pass_on(pool.at[3 + q], 1 - step, q, "gx", me_x, nx, step, 5)
+
+    near = 2 - 2 * (me_y & 1)
+    relay(near)
+    relay(2 - near)
 
     lane = lax.broadcasted_iota(jnp.int32, (8, LANES), 1)
     freq_z = me_x * 8 + (lane >> 4)
@@ -393,7 +397,7 @@
             vmem((256, 2048), bf16),
             pltpu.SemaphoreType.DMA((9,)),
             pltpu.SemaphoreType.DMA((5,)),
-            pltpu.SemaphoreType.DMA((6,)),
+            pltpu.SemaphoreType.DMA((7,)),
         ],
         compiler_params=pltpu.CompilerParams(
             collective_id=0, has_side_effects=True, vmem_limit_bytes=60 * 1024 * 1024

time: 48.2 us -> 48.3 us (level)
  no operation moved by 1% of the time
where the time goes in v5:
time: 48.3 us; the launch traced here: 48.2 us
  Pallas kernels  46.2 us (96%)
  other arithmetic  0.67 us (1%)
  between operations  0.64 us (1%)
  local copies, waits for them, and re-layouts  0.62 us (1%)
    pallas_call x1, Pallas kernels, per_device(): pl.pallas_call(functools.partial(kernel, nx, ny), out_shape=(vmem((256, L...  46.2 us

profile of v5, /device:TPU:1, one launch (start us, length us, event | category | flops | bytes accessed | tf_op | source)
XLA Modules:
  0.0 48.2 jit_solution(15423675886357686460)
XLA Ops:
  0.6 46.2 %shard_map.95 = (f32[256,128]{1,0:T(8,128)S(1)}, f32[3,16,128]{2,1,0:T(8,128)S(1)}) custom-call(f32[128,256]{1,0:T(8,128)} %bitcast.12, f32[6,16,128]{2,1,0:T(8,128)} %bitcast.13, f32[3,16,128]{2,1,0:T(8,128)} %bitcast.14, s32[16,128]{1,0:T(8,128)} %bitcast.15, s32[1,16]{1,0:T(1,128)} %bitcast.17, s32[8,16]{1,0:T(8,128)} %bitcast.16, ...), custom_call_target="tpu_custom_call" | custom-call | tf_op jit(solution)/shard_map/pallas_call | solution.py:362
  46.9 0.6 %copy.13 = f32[3,1,1,2048]{3,2,1,0:T(1,128)} copy(f32[3,1,1,2048]{3,2,1,0:T(1,128)S(1)} %bitcast.10) | data formatting | bytes 49152
  47.5 0.7 %pad_maximum_fusion = f32[128,256]{1,0:T(8,128)} fusion(f32[128,128]{1,0:T(8,128)S(1)} %get-tuple-element.11, f32[128,128]{1,0:T(8,128)S(1)} %get-tuple-element.10), kind=kLoop, calls=%fused_computation | loop fusion | flops 32768 | bytes 262144 | tf_op jit(solution)/shard_map/concatenate | solution.py:415
  (1 shorter events, 0.0 us)
